TPU v7x, 256 devices: a whole 4x4x8 slice. The times are simulated.
256 devices in a mesh: dp: 64 (over x, z, y_lo), seq: 4 (over y_hi, core).
Axes of the slice: x: 4, y: 4 (y_hi: 2, y_lo: 2; y = y_hi * 2 + y_lo), z: 8, core: 2. Of those that a mesh axis runs over, the one named last changes fastest.
Arguments:
- block_input: float32 [128, 512, 768], P('dp', 'seq'), may hold values from -6 to 6
- doc_ids: int32 [128, 512], P('dp'), may hold values from 0 to 2, as said below
- positions: int32 [128, 512], P('dp', 'seq'), may hold values from 0 to 509, as said below
- w_qkv: bfloat16 [768, 2304], P(('dp', 'seq')), may hold values from -0.21875 to 0.21875
- w_out: bfloat16 [768, 768], P(('dp', 'seq')), may hold values from -2.5 to 2.5
- w_in: bfloat16 [768, 2304], P(('dp', 'seq')), may hold values from -0.21875 to 0.21875
- w_down: bfloat16 [768, 1152], P(('dp', 'seq')), may hold values from -0.1875 to 0.1875
- gain_attn: bfloat16 [768], P(('dp', 'seq')), may hold values from 0.099609375 to 1.8984375
- gain_ffn: bfloat16 [768], P(('dp', 'seq')), may hold values from 0.099609375 to 1.8984375
- cotangent: float32 [128, 512, 768], P('dp', 'seq'), may hold values from -16 to 16
Outputs:
- block_output: float32 [128, 512, 768], P('dp', 'seq')
- input_grad: float32 [128, 512, 768], P('dp', 'seq')
- grad_qkv: float32 [768, 2304], P(('dp', 'seq'))
- grad_out: float32 [768, 768], P(('dp', 'seq'))
- grad_in: float32 [768, 2304], P(('dp', 'seq'))
- grad_down: float32 [768, 1152], P(('dp', 'seq'))
- grad_gain_attn: float32 [768], P(('dp', 'seq'))
- grad_gain_ffn: float32 [768], P(('dp', 'seq'))
Inputs may be any that keep to these rules, and one draw needn't show every extreme that they name: `doc_ids`: every sequence holds exactly 3 documents, each a run of tokens, with ids 0 to 2 in order; the boundaries differ from sequence to sequence. `positions`: a token's position counted from the first token of its document.
All inputs are finite; a program needn't handle non-finite values.
Results may differ from a plain program's by a relative error of at most 0.02.
Values may be sent and summed in bfloat16 or wider, within the bound.
A program may use at most 128 MiB of HBM per device.

v0:
```python
import math

import jax
import jax.numpy as jnp
from jax import lax
from jax.sharding import PartitionSpec as P

D = 768
H = 12
HD = 64
FF = 1152


norm_eps = 1e-05
rope_base = 160000.0


def in_one_piece(arrays, axis, dim, along):
    widths = [math.prod(a.shape[along:]) for a in arrays]
    both = jnp.concatenate(
        [a.reshape(*a.shape[:along], w) for a, w in zip(arrays, widths)], axis=along
    )
    filled = lax.all_gather(both, axis, axis=dim, tiled=True)
    blocks = jnp.split(filled, [sum(widths[:k]) for k in range(1, len(widths))], axis=along)
    return tuple(
        (b.reshape(*filled.shape[:along], *a.shape[along:]) for a, b in zip(arrays, blocks))
    )


def sent_together(arrays, axis, dim, along):
    ends, at = ([], 0)
    for a in arrays[:-1]:
        at += a.shape[along]
        ends.append(at)
    both = jnp.concatenate(arrays, axis=along)
    return tuple(
        jnp.split(lax.psum_scatter(both, axis, scatter_dimension=dim, tiled=True), ends, axis=along)
    )


def side_by_side(arrays, axis, dim, along):
    both = jnp.concatenate(arrays, axis=along)
    filled, at, done = (lax.all_gather(both, axis, axis=dim, tiled=True), 0, [])
    for a in arrays:
        done.append(lax.slice_in_dim(filled, at, at + a.shape[along], axis=along))
        at += a.shape[along]
    return tuple(done)


def cut_along(shard, dim, peers):
    shape = shard.shape
    blocks = shard.reshape(*shape[:dim], peers, shape[dim] // peers, *shape[dim + 1 :])
    return jnp.moveaxis(blocks, dim, 0)


def sent_and_summed(shard, axis, dim):
    peers = lax.axis_size(axis)
    blocks = lax.all_to_all(cut_along(shard, dim, peers), axis, 0, 0, tiled=True)
    return jnp.sum(blocks, axis=0)


def in_one_piece_2(arrays, axis, dim, along):
    widths = [a.shape[along] for a in arrays]
    both = jnp.concatenate(arrays, axis=along)
    filled = sent_and_summed(both, axis, dim)
    return tuple(jnp.split(filled, [sum(widths[:k]) for k in range(1, len(widths))], axis=along))


def normalize(matrix):
    center = matrix - jnp.mean(matrix, axis=-1, keepdims=True)
    inverse = lax.rsqrt(jnp.mean(center * center, axis=-1, keepdims=True) + norm_eps)
    return (center * inverse, inverse)


def norm_back(grad_hat, normed, inverse):
    first_mean = jnp.mean(grad_hat, axis=-1, keepdims=True)
    cross_mean = jnp.mean(grad_hat * normed, axis=-1, keepdims=True)
    return (grad_hat - first_mean - normed * cross_mean) * inverse


def rotary_tables(pos_row):
    half_dim = HD // 2
    frequency = rope_base ** (-(jnp.arange(half_dim).astype(jnp.float32) * (2.0 / HD)))
    angles = pos_row.astype(jnp.float32)[:, None] * frequency[None, :]
    return (jnp.cos(angles)[:, None, :], jnp.sin(angles)[:, None, :])


def rotate(matrix, cosine, sine_part):
    half_dim = HD // 2
    first_half = matrix[..., :half_dim]
    second_half = matrix[..., half_dim:]
    return jnp.concatenate(
        [
            first_half * cosine - second_half * sine_part,
            second_half * cosine + first_half * sine_part,
        ],
        axis=-1,
    )


def unrotate(matrix, cosine, sine_part):
    half_dim = HD // 2
    first_half = matrix[..., :half_dim]
    second_half = matrix[..., half_dim:]
    return jnp.concatenate(
        [
            first_half * cosine + second_half * sine_part,
            second_half * cosine - first_half * sine_part,
        ],
        axis=-1,
    )


def gelu_pair(gate_half):
    normal_cdf = 0.5 * (1.0 + lax.erf(gate_half * 0.7071067811865476))
    density = jnp.exp(-0.5 * gate_half * gate_half) * 0.3989422804014327
    return (gate_half * normal_cdf, normal_cdf + gate_half * density)


def forward_dot(left, right):
    return jnp.dot(left, right, preferred_element_type=jnp.float32)


def against_rows(left, right):
    return lax.dot_general(
        left, right, (((1,), (1,)), ((), ())), preferred_element_type=jnp.float32
    )


def over_rows(left, right):
    return lax.dot_general(
        left, right, (((0,), (0,)), ((), ())), preferred_element_type=jnp.float32
    )


def fetch_forward(w_qkv, w_out, w_in, w_down, gain_attn, gain_ffn):
    return in_one_piece((w_qkv, w_out, w_in, w_down, gain_attn, gain_ffn), ("dp", "seq"), 0, 1)


def owner_order(matrix, dp_count, seq_count):
    row_count = matrix.shape[0]
    share = matrix.shape[1] // (dp_count * seq_count)
    return (
        matrix.reshape(row_count, dp_count, seq_count, share)
        .transpose(0, 2, 1, 3)
        .reshape(row_count, matrix.shape[1])
    )


def body(
    block_input, doc_ids, positions, w_qkv, w_out, w_in, w_down, gain_attn, gain_ffn, cotangent
):
    rows_here = block_input.shape[1]
    seq_len = doc_ids.shape[1]
    dp_count = lax.axis_size("dp")
    seq_count = lax.axis_size("seq")
    owned_rows = w_qkv.shape[0]
    local_rows = owned_rows * dp_count
    offset = lax.axis_index("seq") * rows_here
    score_scale = HD ** (-0.5)
    running = (
        jnp.zeros((local_rows, 3 * D), jnp.float32),
        jnp.zeros((local_rows, D), jnp.float32),
        jnp.zeros((local_rows, 2 * FF), jnp.float32),
        jnp.zeros((local_rows, FF), jnp.float32),
    )
    gain_running = (jnp.zeros((D,), jnp.float32), jnp.zeros((D,), jnp.float32))
    own_parts = (
        jnp.zeros(w_qkv.shape, jnp.float32),
        jnp.zeros(w_out.shape, jnp.float32),
        jnp.zeros(w_in.shape, jnp.float32),
        jnp.zeros(w_down.shape, jnp.float32),
    )
    gain_parts = (jnp.zeros(gain_attn.shape, jnp.float32), jnp.zeros(gain_ffn.shape, jnp.float32))
    outputs = []
    input_grads = []
    for step_index in range(block_input.shape[0]):
        whole = fetch_forward(w_qkv, w_out, w_in, w_down, gain_attn, gain_ffn)
        fwd_qkv, fwd_out, fwd_in, fwd_down, fwd_gain_attn, fwd_gain_ffn = whole
        tokens = block_input[step_index]
        grad_top = cotangent[step_index]
        doc_row = doc_ids[step_index]
        doc_here = lax.dynamic_slice_in_dim(doc_row, offset, rows_here)
        cosine, sine_part = rotary_tables(positions[step_index])
        normed_one, inverse_one = normalize(tokens)
        input_one = (normed_one * fwd_gain_attn.astype(jnp.float32)).astype(jnp.bfloat16)
        packed = forward_dot(input_one, fwd_qkv)
        queries = rotate(packed[:, :D].reshape(rows_here, H, HD), cosine, sine_part).astype(
            jnp.bfloat16
        )
        key_here = (
            rotate(packed[:, D : 2 * D].reshape(rows_here, H, HD), cosine, sine_part)
            .astype(jnp.bfloat16)
            .reshape(rows_here, D)
        )
        value_here = packed[:, 2 * D :].astype(jnp.bfloat16)
        key_all, value_all = (
            lax.all_gather(key_here, "seq", axis=0, tiled=True),
            lax.all_gather(value_here, "seq", axis=0, tiled=True),
        )
        key_heads = key_all.reshape(seq_len, H, HD)
        value_heads = value_all.reshape(seq_len, H, HD)
        same_doc = (doc_here[:, None] == doc_row[None, :])[None]
        scores = (
            jnp.einsum("qhd,khd->hqk", queries, key_heads, preferred_element_type=jnp.float32)
            * score_scale
        )
        masked = jnp.where(same_doc, scores, -jnp.inf)
        row_top = jnp.max(masked, axis=-1, keepdims=True)
        log_total = row_top + jnp.log(jnp.sum(jnp.exp(masked - row_top), axis=-1, keepdims=True))
        soft_low = jnp.exp(masked - log_total).astype(jnp.bfloat16)
        attended = (
            jnp.einsum("hqk,khd->qhd", soft_low, value_heads, preferred_element_type=jnp.float32)
            .reshape(rows_here, D)
            .astype(jnp.bfloat16)
        )
        residual = tokens + against_rows(attended, fwd_out)
        normed_two, inverse_two = normalize(residual)
        input_two = (normed_two * fwd_gain_ffn.astype(jnp.float32)).astype(jnp.bfloat16)
        pre_act = forward_dot(input_two, fwd_in)
        gate_half = pre_act[:, :FF]
        up_half = pre_act[:, FF:]
        activated, gate_slope = gelu_pair(gate_half)
        hidden = (activated * up_half).astype(jnp.bfloat16)
        outputs.append(residual + against_rows(hidden, fwd_down))
        back_qkv, back_out, back_in, back_down, back_gain_attn, back_gain_ffn = whole
        grad_low = grad_top.astype(jnp.bfloat16)
        grad_hidden = forward_dot(grad_low, back_down)
        grad_pre = jnp.concatenate(
            [grad_hidden * up_half * gate_slope, grad_hidden * activated], axis=-1
        ).astype(jnp.bfloat16)
        grad_norm_two = against_rows(grad_pre, back_in)
        grad_gain_ffn = jnp.sum(grad_norm_two * normed_two, axis=0)
        grad_resid = grad_top + norm_back(
            grad_norm_two * back_gain_ffn.astype(jnp.float32), normed_two, inverse_two
        )
        resid_low = grad_resid.astype(jnp.bfloat16)
        grad_att = forward_dot(resid_low, back_out).astype(jnp.bfloat16).reshape(rows_here, H, HD)
        row_delta = jnp.sum(
            grad_att.astype(jnp.float32) * attended.reshape(rows_here, H, HD).astype(jnp.float32),
            axis=-1,
        ).T[:, :, None]
        scores_again = (
            jnp.einsum("qhd,khd->hqk", queries, key_heads, preferred_element_type=jnp.float32)
            * score_scale
        )
        soft_again = jnp.exp(jnp.where(same_doc, scores_again, -jnp.inf) - log_total)
        grad_probs = jnp.einsum(
            "qhd,khd->hqk", grad_att, value_heads, preferred_element_type=jnp.float32
        )
        grad_scores = (soft_again * (grad_probs - row_delta) * score_scale).astype(jnp.bfloat16)
        grad_query = jnp.einsum(
            "hqk,khd->qhd", grad_scores, key_heads, preferred_element_type=jnp.float32
        )
        grad_key_all = jnp.einsum(
            "hqk,qhd->khd", grad_scores, queries, preferred_element_type=jnp.float32
        ).reshape(seq_len, D)
        grad_value_all = jnp.einsum(
            "hqk,qhd->khd", soft_low, grad_att, preferred_element_type=jnp.float32
        ).reshape(seq_len, D)
        grad_key_here, grad_value_here = sent_together((grad_key_all, grad_value_all), "seq", 0, 1)
        grad_packed = jnp.concatenate(
            [
                unrotate(grad_query, cosine, sine_part).reshape(rows_here, D),
                unrotate(grad_key_here.reshape(rows_here, H, HD), cosine, sine_part).reshape(
                    rows_here, D
                ),
                grad_value_here,
            ],
            axis=-1,
        ).astype(jnp.bfloat16)
        grad_norm_one = against_rows(grad_packed, back_qkv)
        grad_gain_attn = jnp.sum(grad_norm_one * normed_one, axis=0)
        input_grads.append(
            grad_resid
            + norm_back(grad_norm_one * back_gain_attn.astype(jnp.float32), normed_one, inverse_one)
        )
        row_one, row_two, row_resid, row_grad = (
            lax.all_to_all(
                owner_order(input_one, dp_count, seq_count),
                "seq",
                split_axis=1,
                concat_axis=0,
                tiled=True,
            ),
            lax.all_to_all(
                owner_order(input_two, dp_count, seq_count),
                "seq",
                split_axis=1,
                concat_axis=0,
                tiled=True,
            ),
            lax.all_to_all(
                owner_order(resid_low, dp_count, seq_count),
                "seq",
                split_axis=1,
                concat_axis=0,
                tiled=True,
            ),
            lax.all_to_all(
                owner_order(grad_low, dp_count, seq_count),
                "seq",
                split_axis=1,
                concat_axis=0,
                tiled=True,
            ),
        )
        packed_seq, pre_seq, attended_seq, hidden_seq = side_by_side(
            (grad_packed, grad_pre, attended, hidden), "seq", 0, 1
        )
        terms = (
            over_rows(row_one, packed_seq),
            over_rows(row_resid, attended_seq),
            over_rows(row_two, pre_seq),
            over_rows(row_grad, hidden_seq),
        )
        gain_terms = (grad_gain_attn, grad_gain_ffn)
        running = jax.tree.map(jnp.add, running, terms)
        gain_running = jax.tree.map(jnp.add, gain_running, gain_terms)
    own_parts = in_one_piece_2((running[0], running[1], running[2], running[3]), "dp", 0, 1)
    gain_parts = (
        lax.psum_scatter(gain_running[0], ("dp", "seq"), scatter_dimension=0, tiled=True),
        lax.psum_scatter(gain_running[1], ("dp", "seq"), scatter_dimension=0, tiled=True),
    )
    return (
        jnp.stack(outputs),
        jnp.stack(input_grads),
        own_parts[0],
        own_parts[1],
        own_parts[2],
        own_parts[3],
        gain_parts[0],
        gain_parts[1],
    )


def solution(mesh):
    return jax.shard_map(
        body,
        mesh=mesh,
        in_specs=(
            P("dp", "seq", None),
            P("dp", None),
            P("dp", "seq"),
            P(("dp", "seq"), None),
            P(("dp", "seq"), None),
            P(("dp", "seq"), None),
            P(("dp", "seq"), None),
            P(("dp", "seq")),
            P(("dp", "seq")),
            P("dp", "seq", None),
        ),
        out_specs=(
            P("dp", "seq", None),
            P("dp", "seq", None),
            P(("dp", "seq"), None),
            P(("dp", "seq"), None),
            P(("dp", "seq"), None),
            P(("dp", "seq"), None),
            P(("dp", "seq")),
            P(("dp", "seq")),
        ),
        check_vma=False,
    )
```

profile of v0, /device:TPU:1, one launch (start us, length us, event | category | flops | bytes accessed | tf_op | source)
XLA Modules:
  0.0 1065.7 jit_solution(9702997083633565786)
XLA Ops:
  16.4 425.0 %all-gather.9.cloned.1.call-done = bf16[256,3,6530]{2,1,0:T(4,128)(2,1)} async-done(((bf16[1,3,6530]{2,1,0:T(4,128)(2,1)}), bf16[256,3,6530]{2,1,0:T(4,128)(2,1)}) %all-gather.9.cloned.1.call-update) | async-done | bytes 10030096 | tf_op jit(solution)/shard_map/all_gather | solution.py:23
  441.4 24.2 %reshape.524 = bf16[768,6530]{1,0:T(8,128)(2,1)} reshape(bf16[256,3,6530]{2,1,0:T(4,128)(2,1)} %all-gather.9.cloned.1.call-done) | data formatting | bytes 20060160
  474.9 12.1 %all_gather.26 = bf16[512,768]{0,1:T(8,128)(2,1)} all-gather(bf16[128,768]{0,1:T(8,128)(2,1)S(1)} %bitcast.287), channel_id=1, replica_groups=mesh['dp'=64,'seq'=4] {'seq'}, dimensions={0}, use_global_device_ids=true | all-gather | bytes 983040 | tf_op jit(solution)/shard_map/all_gather | solution.py:198
  487.1 10.2 all_gather.25
  499.6 10.4 all_gather.24
  510.0 11.3 %all_gather.23 = bf16[512,768]{1,0:T(8,128)(2,1)} all-gather(bf16[128,768]{1,0:T(8,128)(2,1)} %slice.321), channel_id=1, replica_groups=mesh['dp'=64,'seq'=4] {'seq'}, dimensions={0}, use_global_device_ids=true | all-gather | bytes 983040 | tf_op jit(solution)/shard_map/all_gather | solution.py:199
  547.3 4.1 fusion.104
  584.9 21.6 %reduce-scatter.3.cloned.1.call-done = f32[128,1536]{1,0:T(8,128)} async-done(((f32[512,1536]{1,0:T(8,128)}), f32[128,1536]{1,0:T(8,128)}) %reduce-scatter.3.cloned.1.call-update) | async-done | bytes 786448 | tf_op jit(solution)/shard_map/reduce_scatter | solution.py:37
  619.5 39.6 %reduce-scatter.5.cloned.1.call-done = f32[128,1536]{1,0:T(8,128)} async-done(((f32[512,1536]{1,0:T(8,128)}), f32[128,1536]{1,0:T(8,128)}) %reduce-scatter.5.cloned.1.call-update) | async-done | bytes 786448 | tf_op jit(solution)/shard_map/reduce_scatter | solution.py:37
  678.2 4.2 all-to-all-start.4
  690.9 4.2 all-to-all-start.5
  695.1 25.0 %all-gather.5.cloned.1.call-done = bf16[512,6528]{1,0:T(8,128)(2,1)} async-done(((bf16[128,6528]{1,0:T(8,128)(2,1)}), bf16[512,6528]{1,0:T(8,128)(2,1)}) %all-gather.5.cloned.1.call-update) | async-done | bytes 6684688 | tf_op jit(solution)/shard_map/all_gather | solution.py:43
  727.3 49.2 %all-gather.7.cloned.1.call-done = bf16[512,6528]{1,0:T(8,128)(2,1)} async-done(((bf16[128,6528]{1,0:T(8,128)(2,1)}), bf16[512,6528]{1,0:T(8,128)(2,1)}) %all-gather.7.cloned.1.call-update) | async-done | bytes 6684688 | tf_op jit(solution)/shard_map/all_gather | solution.py:43
  788.8 4.2 all-to-all-start.7
  799.7 4.2 all-to-all-start.2
  805.9 4.0 all-to-all-done.2
  809.9 4.8 all-to-all-start.3
  817.0 3.8 all-to-all-done.3
  820.8 4.2 all-to-all-start.1
  836.4 8.0 reshape.519
  844.4 10.6 all-to-all-start.8
  858.5 4.7 multiply_reduce_fusion.3
  863.3 181.9 %all-reduce.2 = (f32[768]{0:T(1024)S(1)}, f32[768]{0:T(1024)S(1)}) all-reduce(f32[768]{0:T(1024)S(1)} %add.173, f32[768]{0:T(1024)S(1)} %add.174), channel_id=4, replica_groups=mesh['dp'=64,'seq'=4] {'dp','seq'}, use_global_device_ids=true, to_apply=%region_27.28.clone | all-reduce | flops 1536 | bytes 12288
  1053.0 3.8 reduce_sum.245
  (391 shorter events, 174.5 us)
Async XLA Ops:
  7.2 434.2 %all-gather.9.cloned.1.call-start = ((), (), s32[]{:S(2)}) async-start(), calls=%async_computation.15 | async-start | bytes 13684736 | tf_op jit(solution)/shard_map/all_gather | solution.py:23
  10.2 596.3 %reduce-scatter.3.cloned.1.call-start = ((), (), s32[]{:S(2)}) async-start(), calls=%async_computation.11 | async-start | bytes 3932160 | tf_op jit(solution)/shard_map/reduce_scatter | solution.py:37
  13.1 454.4 %copy-start.81 = (f32[128]{0:T(128)}, f32[128]{0:T(128)S(1)}, u32[]{:S(2)}) copy-start(f32[128]{0:T(128)S(1)} %get-tuple-element.108) | copy-start | bytes 1540
  13.1 457.2 %copy-start.83 = (f32[128]{0:T(128)}, f32[128]{0:T(128)S(1)}, u32[]{:S(2)}) copy-start(f32[128]{0:T(128)S(1)} %get-tuple-element.109) | copy-start | bytes 1540
  14.5 455.8 %copy-start.87 = (f32[128]{0:T(128)}, f32[128]{0:T(128)S(1)}, u32[]{:S(2)}) copy-start(f32[128]{0:T(128)S(1)} %add_rsqrt_fusion.3) | copy-start | bytes 1540
  14.5 453.0 %copy-start.89 = (f32[128]{0:T(128)}, f32[128]{0:T(128)S(1)}, u32[]{:S(2)}) copy-start(f32[128]{0:T(128)S(1)} %add_rsqrt_fusion.1) | copy-start | bytes 1540
  15.5 458.6 %copy-start.70 = (f32[128,32]{0,1:T(8,128)}, f32[128,32]{0,1:T(8,128)S(1)}, u32[]{:S(2)}) copy-start(f32[128,32]{0,1:T(8,128)S(1)} %get-tuple-element.96) | copy-start | bytes 49156
  15.5 483.2 %copy-start.71 = (f32[128,32]{0,1:T(8,128)}, f32[128,32]{0,1:T(8,128)S(1)}, u32[]{:S(2)}) copy-start(f32[128,32]{0,1:T(8,128)S(1)} %get-tuple-element.89) | copy-start | bytes 49156
  15.5 483.2 %copy-start.73 = (f32[128,32]{0,1:T(8,128)}, f32[128,32]{0,1:T(8,128)S(1)}, u32[]{:S(2)}) copy-start(f32[128,32]{0,1:T(8,128)S(1)} %get-tuple-element.90) | copy-start | bytes 49156
  16.4 509.9 %copy-start.38 = (pred[128,512]{1,0:T(8,128)(4,1)}, pred[128,512]{1,0:T(8,128)(4,1)S(1)}, u32[]{:S(2)}) copy-start(pred[128,512]{1,0:T(8,128)(4,1)S(1)} %broadcast_compare_fusion.1) | copy-start | bytes 196612
  16.4 451.1 %copy-start.4 = (f32[2,128,768]{2,1,0:T(8,128)S(1)}, f32[2,128,768]{2,1,0:T(8,128)}, u32[]{:S(2)}) copy-start(f32[2,128,768]{2,1,0:T(8,128)} %param.10) | copy-start | bytes 2359300
  561.4 97.7 %reduce-scatter.5.cloned.1.call-start = ((), (), s32[]{:S(2)}) async-start(), calls=%async_computation.12 | async-start | bytes 3932160 | tf_op jit(solution)/shard_map/reduce_scatter | solution.py:37
  582.6 137.5 %all-gather.5.cloned.1.call-start = ((), (), s32[]{:S(2)}) async-start(), calls=%async_computation.13 | async-start | bytes 8355840 | tf_op jit(solution)/shard_map/all_gather | solution.py:43
  617.9 158.5 %all-gather.7.cloned.1.call-start = ((), (), s32[]{:S(2)}) async-start(), calls=%async_computation.14 | async-start | bytes 8355840 | tf_op jit(solution)/shard_map/all_gather | solution.py:43
  678.2 12.7 %all-to-all-start.4 = ((bf16[128,4,192]{0,2,1:T(8,128)(2,1)}), bf16[128,4,192]{0,2,1:T(8,128)(2,1)S(1)}, u32[]{:S(2)}, u32[]{:S(2)}) async-start(bf16[128,4,192]{0,2,1:T(8,128)(2,1)} %copy.141), calls=%async_computation.6 | async-start | bytes 393216 | tf_op jit(solution)/shard_map/all_to_all | solution.py:286
  690.9 32.8 %all-to-all-start.5 = ((bf16[128,4,192]{0,2,1:T(8,128)(2,1)}), bf16[128,4,192]{0,2,1:T(8,128)(2,1)S(1)}, u32[]{:S(2)}, u32[]{:S(2)}) async-start(bf16[128,4,192]{0,2,1:T(8,128)(2,1)} %copy.145), calls=%async_computation.7 | async-start | bytes 393216 | tf_op jit(solution)/shard_map/all_to_all | solution.py:286
  723.7 55.6 %all-to-all-start = ((bf16[128,4,192]{0,2,1:T(8,128)(2,1)}), bf16[128,4,192]{0,2,1:T(8,128)(2,1)S(1)}, u32[]{:S(2)}, u32[]{:S(2)}) async-start(bf16[128,4,192]{0,2,1:T(8,128)(2,1)} %copy.119), calls=%async_computation.2 | async-start | bytes 393216 | tf_op jit(solution)/shard_map/all_to_all | solution.py:279
  779.3 9.6 all-to-all-start.6
  788.8 10.2 all-to-all-start.7
  799.7 10.2 all-to-all-start.2
  809.9 10.9 %all-to-all-start.3 = ((bf16[128,4,192]{0,2,1:T(8,128)(2,1)}), bf16[128,4,192]{0,2,1:T(8,128)(2,1)}, u32[]{:S(2)}, u32[]{:S(2)}) async-start(bf16[128,4,192]{0,2,1:T(8,128)(2,1)} %copy.137), calls=%async_computation.5 | async-start | bytes 393216 | tf_op jit(solution)/shard_map/all_to_all | solution.py:293
  820.8 10.2 all-to-all-start.1
  844.4 208.6 %all-to-all-start.8 = ((f32[64,3,6528]{2,1,0:T(4,128)}), f32[64,3,6528]{2,1,0:T(4,128)}, u32[]{:S(2)}, u32[]{:S(2)}) async-start(f32[64,3,6528]{2,1,0:T(4,128)} %reshape.519), calls=%async_computation.10 | async-start | bytes 13369344 | tf_op jit(solution)/shard_map/all_to_all | solution.py:58
  858.5 190.1 %copy-start.12 = (f32[128,768]{1,0:T(8,128)S(1)}, f32[128,768]{1,0:T(8,128)}, u32[]{:S(2)}) copy-start(f32[128,768]{1,0:T(8,128)} %copy-done.11) | copy-start | bytes 1179652
  (90 other events, 646.3 us)
Sparse Core Ops, SparseCore 0:
  10.5 430.8 all-gather.8
  561.5 45.0 reduce-scatter.2
  609.6 49.4 reduce-scatter.4
  660.8 59.2 all-gather.4
  721.7 54.6 all-gather.6
where the time goes:
time: 1070 us
  waiting for transfers between devices  580 us (54%)
  blocking collectives  226 us (21%)
  local copies, waits for them, and re-layouts  93.9 us (9%)
  matrix products  71.9 us (7%)
  starting transfers between devices  43.8 us (4%)
  other arithmetic  34.1 us (3%)
  between operations  15.9 us (1%)
    all_gather x1, waiting for transfers between devices, in_one_piece(): filled = lax.all_gather(both, axis, axis=dim, tiled=True)  425 us
    unnamed x1, blocking collectives  182 us
    all_gather x2, waiting for transfers between devices, side_by_side(): filled, at, done = (lax.all_gather(both, axis, axis=dim, tiled=True), 0, [])  74.2 us
    reduce_scatter x2, waiting for transfers between devices, sent_together(): lax.psum_scatter(both, axis, scatter_dimension=dim, tiled=True)  61.2 us
    unnamed x215, local copies, waits for them, and re-layouts  47.2 us
    all_gather x2, blocking collectives, body(): lax.all_gather(key_here, 'seq', axis=0, tiled=True)  22.5 us
    dot_general x8, matrix products, over_rows(): lax.dot_general(left, right, (((0,), (0,)), ((), ())), preferred_element_...  22.4 us
    all_gather x2, blocking collectives, body(): lax.all_gather(value_here, 'seq', axis=0, tiled=True)  21.5 us
  transfers between devices with their start and end apart: 14, of which 11 were waited for; matrix products, arithmetic and copies ran while one was open for 9% of the time, Pallas kernels for 0%

commit v1 on v0

v1 whole, which is shorter than its diff:
```python
import math


import jax
import jax.numpy as jnp
from jax import lax
from jax.experimental import pallas as pl
from jax.experimental.pallas import tpu as pltpu
from jax.sharding import PartitionSpec as P

D = 768
H = 12
HD = 64
FF = 1152
NW = 6528
NC = 6656
START = (0, 2560)
WIDE = (640, 1024)
SIZE = (32, 48)
MANY = (5, 8)
CUT = (((0, 384), (384, 256)), ((0, 512), (512, 512)))
MESH = pl.DeviceIdType.MESH
f32 = jnp.float32
bf16 = jnp.bfloat16


def coords():
    dp = lax.axis_index("dp")
    sq = lax.axis_index("seq")
    x = lax.div(dp, 16)
    z = lax.rem(lax.div(dp, 2), 8)
    ylo = lax.rem(dp, 2)
    yhi = lax.div(sq, 2)
    c = lax.rem(sq, 2)
    return x, yhi * 2 + ylo, z, c


def device(x, y, z, c):
    return (x * 16 + z * 2 + lax.rem(y, 2), lax.div(y, 2) * 2 + c)


def remote(src, dst, send, recv, to):
    return pltpu.make_async_remote_copy(
        src_ref=src, dst_ref=dst, send_sem=send, recv_sem=recv, device_id=to, device_id_type=MESH
    )


def greet(x, y, z, c):
    barrier = pltpu.get_barrier_semaphore()
    peers = [device(x, y, z, 1 - c)]
    peers += [device(lax.rem(x + k, 4), y, z, c) for k in (1, 3)]
    peers += [device(x, lax.rem(y + k, 4), z, c) for k in (1, 2, 3)]
    for to in peers:
        pl.semaphore_signal(barrier, inc=1, device_id=to, device_id_type=MESH)

    def hail(k, _):
        pl.semaphore_signal(
            barrier, inc=1, device_id=device(x, y, lax.rem(z + k, 8), c), device_id_type=MESH
        )
        return 0

    lax.fori_loop(1, 8, hail, 0)
    pl.semaphore_wait(barrier, len(peers) + 7)


class Ring:
    def __init__(self, me, to, block, send, recv, first):
        self.right = lax.rem(me + 1, 4)
        self.left = lax.rem(me + 3, 4)
        self.far = lax.rem(me + 2, 4)
        self.me, self.to, self.block, self.first = me, to, block, first
        self.send, self.recv = send, recv
        self.started = []

    def go(self, slot, i, h, to, src=None):
        copy = remote(
            self.block(i, h) if src is None else src,
            self.block(i, h),
            self.send.at[slot],
            self.recv.at[slot],
            self.to(to),
        )
        copy.start()
        self.started.append(copy)

    def begin(self):
        mine = self.first
        self.go(0, self.me, 0, self.right, mine(0) if mine else None)
        self.go(1, self.me, 1, self.left, mine(1) if mine else None)
        self.go(2, self.me, 1, self.right, mine(1) if mine else None)
        self.go(3, self.me, 0, self.left, mine(0) if mine else None)

    def got(self, slot, i, h):
        remote(
            self.block(i, h), self.block(i, h), self.send.at[slot], self.recv.at[slot], self.to(self.right)
        ).wait_recv()

    def forward(self):
        self.got(0, self.left, 0)
        self.go(4, self.left, 0, self.right)
        self.got(1, self.right, 1)
        self.go(5, self.right, 1, self.left)

    def near(self):
        self.got(2, self.left, 1)
        self.got(3, self.right, 0)

    def last(self):
        self.got(4, self.far, 0)
        self.got(5, self.far, 1)

    def sent(self):
        for copy in self.started:
            copy.wait_send()


class Reduce:
    def __init__(self, me, to, block, land, send, recv):
        self.right = lax.rem(me + 1, 4)
        self.left = lax.rem(me + 3, 4)
        self.far = lax.rem(me + 2, 4)
        self.me, self.to, self.block, self.land = me, to, block, land
        self.send, self.recv = send, recv
        self.started = []

    def go(self, slot, i, h, to):
        copy = remote(
            self.block(i, h), self.land(slot, h), self.send.at[slot], self.recv.at[slot], self.to(to)
        )
        copy.start()
        self.started.append(copy)

    def got(self, slot, h):
        at = self.land(slot, h)
        remote(at, at, self.send.at[slot], self.recv.at[slot], self.to(self.right)).wait_recv()

    def one(self):
        self.go(0, self.far, 0, self.right)
        self.go(1, self.far, 1, self.left)

    def two(self):
        self.go(3, self.right, 1, self.right)

    def three(self):
        self.go(4, self.left, 0, self.left)

    def pass_right(self):
        self.got(0, 0)
        add_into(self.block(self.right, 0), self.land(0, 0))
        self.go(2, self.right, 0, self.right)

    def pass_left(self):
        self.got(1, 1)
        add_into(self.block(self.left, 1), self.land(1, 1))
        self.go(5, self.left, 1, self.left)

    def landed(self):
        for slot, h in ((3, 1), (4, 0), (2, 0), (5, 1)):
            self.got(slot, h)

    def sent(self):
        for copy in self.started:
            copy.wait_send()


def add_into(at, more):
    def row(r, _):
        at[r] = (at[r].astype(f32) + more[r].astype(f32)).astype(bf16)
        return 0

    lax.fori_loop(0, 3, row, 0)


def normalize(matrix):
    center = matrix - jnp.mean(matrix, axis=-1, keepdims=True)
    inverse = lax.rsqrt(jnp.mean(center * center, axis=-1, keepdims=True) + 1e-05)
    return center * inverse, inverse


def norm_back(grad_hat, normed, inverse):
    first_mean = jnp.mean(grad_hat, axis=-1, keepdims=True)
    cross_mean = jnp.mean(grad_hat * normed, axis=-1, keepdims=True)
    return (grad_hat - first_mean - normed * cross_mean) * inverse


def dot(left, right):
    return jnp.dot(left, right, preferred_element_type=f32)


def dot_rows(left, right):
    return lax.dot_general(left, right, (((1,), (1,)), ((), ())), preferred_element_type=f32)


def dot_over(left, right):
    return lax.dot_general(left, right, (((0,), (0,)), ((), ())), preferred_element_type=f32)


def tiles(count, width, step):
    def one(n, _):
        step(pl.ds(pl.multiple_of(n * width, width), width))
        return 0

    lax.fori_loop(0, count, one, 0)


def shifted(at, by):
    return pl.ds(pl.multiple_of(at.start + by, 128), at.size)


def block_kernel(
    blk, tok, cot, doc, r_out, o_out, g_out,
    sb_a, sb_b, sf_a, sf_b, give_x, give_g, xs, gs, w, d_w, half, land2_a, land2_b, land1_a, land1_b, zbuf_a, zbuf_b, res_a, res_b,
    d_out, d_tok, tok_half, tok_sum,
    cosine, sine, inner, tok_in, normed_all, inverse_all, in_all, q, k, v, bias, soft, att, first_part,
    normed_two, in_two, top, hidden, d_pre, d_two, back_two, resid, d_att, d_q, d_kv, d_one,
    in_all_t, in_own_t, in_two_t, resid_t, top_t, out_low,
    pair_s, pair_r, z_s, z_r, ring_s, ring_r, core_s, core_r, loc, tok_s, tok_r,
    half_s, half_r, back_s, back_r, y_s, y_r, fin_s, fin_r, ret_s, ret_r, keep_s,
):
    x, y, z, c = coords()
    hi = lax.div(y, 2)
    greet(x, y, z, c)
    sib = device(x, y, z, 1 - c)
    far = device(x, lax.rem(y + 2, 4), z, c)
    along_x = lambda i: device(i, y, z, c)
    along_y = lambda i: device(x, i, z, c)
    b_own = 2 * hi + c
    b_far = 2 * (1 - hi) + c

    sb, sf, zbuf, res = (sb_a, sb_b), (sf_a, sf_b), (zbuf_a, zbuf_b), (res_a, res_b)
    part = (pl.ds(0, 32), pl.ds(32, 48))

    def owner(g, o, n=1):
        return pl.ds(pl.multiple_of(o * SIZE[g], SIZE[g]), SIZE[g] * n)

    def cols(g, core, p, at=0, n=None):
        n = WIDE[g] if n is None else n
        return pl.ds(pl.multiple_of(START[g] + core * 2 * WIDE[g] + p * WIDE[g] + at, 128), n)

    mine, pair = [], []
    for g in range(2):
        at = sb[g].at[owner(g, z * 2 + c)]
        mine.append(pltpu.make_async_copy(blk.at[c, part[g]], at, loc.at[g]))
        mine[g].start()
        pair.append(remote(blk.at[1 - c, part[g]], at, pair_s.at[g], pair_r.at[g], sib))
        pair[g].start()

    def spread(g):
        mine[g].wait()
        pair[g].wait()
        at = sb[g].at[owner(g, z * 2, 2)]

        def push(n, _):
            remote(at, at, z_s.at[g, n], z_r.at[g, n], device(x, y, lax.rem(z + n, 8), c)).start()
            return 0

        lax.fori_loop(1, 8, push, 0)

    give_x[...] = tok[1 - hi].astype(bf16)
    give_g[...] = cot[1 - hi].astype(bf16)
    xs[b_own] = tok[hi].astype(bf16)
    gs[hi] = cot[hi].astype(bf16)
    spread(0)
    spread(1)
    give = [
        remote(give_x, xs.at[b_own], tok_s.at[0], tok_r.at[0], far),
        remote(give_g, gs.at[hi], tok_s.at[1], tok_r.at[1], far),
        remote(xs.at[b_own], xs.at[b_own], tok_s.at[2], tok_r.at[2], sib),
    ]
    for copy in give:
        copy.start()

    lane = lax.broadcasted_iota(jnp.int32, (1, 128), 1)
    low = (lane & 63) < 32
    heads = (lane < 64, lane >= 64)
    own = [pl.ds(pl.multiple_of(c * 128 + j * 256, 128), 128) for j in range(2)]
    local = [pl.ds(j * 128, 128) for j in range(2)]

    p_row = lax.broadcasted_iota(jnp.int32, (1, D), 1)
    o, gy, gx = p_row & 15, (p_row >> 4) & 3, (p_row >> 6) & 3
    holder = ((gx * 8 + (o >> 1)) * 2 + (gy & 1)) * 4 + (gy >> 1) * 2 + (o & 1)
    feature = holder * 3 + (p_row >> 8)
    inner[...] = (lax.broadcasted_iota(jnp.int32, (D, D), 0) == feature).astype(f32).astype(bf16)

    ids = doc[pl.ds(hi, 1), :].astype(f32)
    rows8 = jnp.where(lax.broadcasted_iota(jnp.int32, (8, 512), 0) == 0, ids, 0.0)
    doc_col = dot_over(rows8.astype(bf16), jnp.ones((8, 128), bf16))
    begin_one = jnp.sum(jnp.where(ids < 0.5, 1.0, 0.0), axis=-1, keepdims=True)
    begin_two = jnp.sum(jnp.where(ids < 1.5, 1.0, 0.0), axis=-1, keepdims=True)
    begin = jnp.where(doc_col > 1.5, begin_two, jnp.where(doc_col > 0.5, begin_one, 0.0))
    place = lax.broadcasted_iota(jnp.int32, (512, 128), 0).astype(f32) - begin
    turns = (lane & 31).astype(f32) * (2.0 / HD)
    angles = place * jnp.exp(turns * -math.log(160000.0))
    cosine[...] = jnp.cos(angles)
    sine[...] = jnp.where(low, -jnp.sin(angles), jnp.sin(angles))
    inverse_all[...] = doc_col
    for j in range(2):
        bias[local[j], :] = jnp.where(inverse_all[own[j], 0:1] == ids, 0.0, -1e30)

    def tile_up(g):
        def arrive(n, _):
            there = sb[g].at[owner(g, lax.rem(z + 8 - n, 8) * 2, 2)]
            remote(there, there, z_s.at[g, n], z_r.at[g, n], device(x, y, lax.rem(z + n, 8), c)).wait()
            return 0

        lax.fori_loop(1, 8, arrive, 0)
        sf[g][...] = sb[g][...].astype(f32)
        for p in range(2):
            for r in range(3):
                for t in range(MANY[g]):
                    line = (r * 2 + p) * MANY[g] + t
                    w[r, x, y, :, cols(g, c, p, t * 128, 128)] = sf[g][
                        pl.ds(line, 16, stride=SIZE[g]), :
                    ].astype(bf16)

    def one_step(g):
        return (
            Ring(x, along_x, lambda i, h: w.at[:, i, y, :, cols(g, c, 0, *CUT[g][h])],
                 ring_s.at[4 * g], ring_r.at[4 * g], None),
            Ring(y, along_y, lambda i, h: w.at[:, x, i, :, cols(g, c, 1, *CUT[g][h])],
                 ring_s.at[4 * g + 1], ring_r.at[4 * g + 1], None),
        )

    def two_step(g):
        return (
            Ring(y, along_y, lambda i, h: w.at[:, pl.ds(2 * h, 2), i, :, cols(g, c, 0)],
                 ring_s.at[4 * g + 2], ring_r.at[4 * g + 2], None),
            Ring(x, along_x, lambda i, h: w.at[:, i, pl.ds(2 * h, 2), :, cols(g, c, 1)],
                 ring_s.at[4 * g + 3], ring_r.at[4 * g + 3], None),
        )

    def piece(ref, p, i, at):
        return ref.at[:, :, i, :, at] if p == 0 else ref.at[:, i, :, :, at]

    handed = []

    def hand(g, ring, p, n, i):
        at = piece(w, p, i, cols(g, c, p))
        copy = remote(at, at, core_s.at[g, p, n], core_r.at[g, p, n], sib)
        copy.start()
        handed.append(copy)

    def taken(g, rings):
        for p in range(2):
            ring = rings[p]
            for n, i in enumerate((ring.me, ring.left, ring.right, ring.far)):
                at = piece(w, p, i, cols(g, 1 - c, p))
                remote(at, at, core_s.at[g, p, n], core_r.at[g, p, n], sib).wait_recv()

    def enter(b):
        rows = pl.ds(pl.multiple_of(b * 128, 128), 128)
        tokens = dot(xs[b], inner[...])
        tok_in[rows, :] = tokens.astype(bf16)
        normed, inverse = normalize(tokens)
        normed_all[rows, :] = normed
        inverse_all[rows, :] = jnp.broadcast_to(inverse, (128, 128))

    a_one, b_one, a_two, b_two = one_step(0), one_step(1), two_step(0), two_step(1)
    tile_up(0)
    for ring in a_one:
        ring.begin()
    tile_up(1)
    for ring in b_one:
        ring.begin()
    for ring in a_one:
        ring.forward()
    for ring in a_one:
        ring.near()
        ring.last()
    for ring in a_two:
        ring.begin()
    for p in range(2):
        hand(0, a_two[p], p, 0, a_two[p].me)
    for ring in b_one:
        ring.forward()
    enter(b_own)

    for n, at in enumerate((xs.at[b_far], gs.at[1 - hi])):
        remote(at, at, tok_s.at[n], tok_r.at[n], far).wait_recv()
    passed = remote(xs.at[b_far], xs.at[b_far], tok_s.at[3], tok_r.at[3], sib)
    passed.start()
    at = xs.at[2 * hi + 1 - c]
    remote(at, at, tok_s.at[2], tok_r.at[2], sib).wait_recv()
    for ring in b_one:
        ring.near()
        ring.last()
    for ring in a_two:
        ring.forward()
    for ring in b_two:
        ring.begin()
    for p in range(2):
        hand(1, b_two[p], p, 0, b_two[p].me)
    enter(b_far)
    for p in range(2):
        a_two[p].near()
        hand(0, a_two[p], p, 1, a_two[p].left)
        hand(0, a_two[p], p, 2, a_two[p].right)
    enter(2 * hi + 1 - c)
    for p in range(2):
        a_two[p].last()
        hand(0, a_two[p], p, 3, a_two[p].far)
    at = xs.at[2 * (1 - hi) + 1 - c]
    remote(at, at, tok_s.at[3], tok_r.at[3], sib).wait_recv()
    enter(2 * (1 - hi) + 1 - c)
    for j in range(2):
        top[local[j], :] = dot(gs[j], inner[...]).astype(bf16)
    top_t[...] = top[...].T
    taken(0, a_two)

    def wide(at):
        return w[:, :, :, :, at].reshape(D, at.size)

    def row_tile(n, at):
        return w[n, :, :, :, at].reshape(256, at.size)

    def put(at, value):
        d_w[:, :, :, :, at] = value.astype(bf16).reshape(3, 4, 4, 16, at.size)

    def turn(a, rows, sign):
        swap = jnp.where(low, pltpu.roll(a, 96, 1), pltpu.roll(a, 32, 1))
        return a * cosine[rows, :] + swap * (sign * sine[rows, :])

    pick = (
        lax.broadcasted_iota(jnp.int32, (8, 128), 0) == lax.broadcasted_iota(jnp.int32, (8, 128), 1)
    ).astype(f32).astype(bf16)
    gains = dot_rows(pick, wide(pl.ds(0, 128)))
    gain_one, gain_two = gains[0:1], gains[1:2]

    def scale(rows):
        in_all[rows, :] = (normed_all[rows, :] * gain_one).astype(bf16)

    tiles(4, 128, scale)

    def project(n):
        kk = dot(in_all[...], wide(shifted(n, 896)))
        k[:, n] = turn(kk, pl.ds(0, 512), 1.0).astype(bf16)
        v[:, n] = dot(in_all[...], wide(shifted(n, 1664))).astype(bf16)
        for j in range(2):
            q[local[j], n] = turn(dot(in_all[own[j], :], wide(shifted(n, 128))), own[j], 1.0).astype(bf16)

    tiles(6, 128, project)
    for ring in b_two:
        ring.forward()

    def attend(n, _):
        at = pl.ds(pl.multiple_of(n * 128, 128), 128)
        q2, k2, v2 = q[:, at], k[:, at], v[:, at]
        parts = []
        for h in range(2):
            score = dot_rows(jnp.where(heads[h], q2, jnp.zeros_like(q2)), k2) * 0.125 + bias[...]
            raised = jnp.exp(score - jnp.max(score, axis=-1, keepdims=True))
            prob = (raised * (1.0 / jnp.sum(raised, axis=-1, keepdims=True))).astype(bf16)
            soft[2 * n + h] = prob
            parts.append(dot(prob, v2))
        att[:, at] = jnp.where(heads[0], parts[0], parts[1]).astype(bf16)
        return 0

    lax.fori_loop(0, 3, attend, 0)
    for p in range(2):
        b_two[p].near()
        hand(1, b_two[p], p, 1, b_two[p].left)
        hand(1, b_two[p], p, 2, b_two[p].right)
    lax.fori_loop(3, 6, attend, 0)
    for p in range(2):
        b_two[p].last()
        hand(1, b_two[p], p, 3, b_two[p].far)
    taken(1, b_two)

    def leave(n, _):
        first_part[:, pl.ds(pl.multiple_of(n * 256, 256), 256)] = dot_rows(att[...], row_tile(n, pl.ds(2432, 768)))
        return 0

    lax.fori_loop(0, 3, leave, 0)
    inverse_two = []
    for j in range(2):
        residual = tok_in[own[j], :].astype(f32) + first_part[local[j], :]
        normed, inverse = normalize(residual)
        normed_two[local[j], :] = normed
        inverse_two.append(inverse)
        in_two[local[j], :] = (normed * gain_two).astype(bf16)

    def feed(n):
        gate = dot(in_two[...], wide(shifted(n, 3200)))
        up = dot(in_two[...], wide(shifted(n, 4352)))
        back = dot(top[...], wide(shifted(n, 5504)))
        cdf = 0.5 * (1.0 + lax.erf(gate * 0.7071067811865476))
        slope = cdf + gate * (jnp.exp(-0.5 * gate * gate) * 0.3989422804014327)
        act = gate * cdf
        hidden[:, n] = (act * up).astype(bf16)
        d_pre[:, n] = (back * up * slope).astype(bf16)
        d_pre[:, shifted(n, 1152)] = (back * act).astype(bf16)

    tiles(9, 128, feed)

    def finish(n, _):
        at = pl.ds(pl.multiple_of(n * 256, 256), 256)
        out_low[:, at] = (first_part[:, at] + dot_rows(hidden[...], row_tile(n, pl.ds(5504, 1152)))).astype(bf16)
        d_two[:, at] = dot_rows(d_pre[...], row_tile(n, pl.ds(3200, 2304)))
        return 0

    lax.fori_loop(0, 3, finish, 0)
    for j in range(2):
        grad, normed = d_two[local[j], :], normed_two[local[j], :]
        back = norm_back(grad * gain_two, normed, inverse_two[j])
        back_two[local[j], :] = back
        resid[local[j], :] = (top[local[j], :].astype(f32) + back).astype(bf16)

    in_two_t[...] = in_two[...].T
    resid_t[...] = resid[...].T

    def weights_o(n):
        put(shifted(n, 2432), dot(resid_t[...], att[:, n]))

    def weights_in(n):
        put(shifted(n, 3200), dot(in_two_t[...], d_pre[:, n]))

    def weights_down(n):
        put(shifted(n, 5504), dot(top_t[...], hidden[:, n]))

    tiles(3, 256, weights_o)
    tiles(9, 256, weights_in)
    tiles(3, 384, weights_down)

    land2, land1 = (land2_a, land2_b), (land1_a, land1_b)

    def back_two_step(g):
        return (
            Reduce(y, along_y, lambda i, h: d_w.at[:, 2 * h : 2 * h + 2, i, :, cols(g, c, 0)],
                   lambda s, h: land2[g].at[0, s], back_s.at[4 * g + 2], back_r.at[4 * g + 2]),
            Reduce(x, along_x, lambda i, h: d_w.at[:, i, 2 * h : 2 * h + 2, :, cols(g, c, 1)],
                   lambda s, h: land2[g].at[1, s], back_s.at[4 * g + 3], back_r.at[4 * g + 3]),
        )

    def back_one_step(g):
        return (
            Reduce(x, along_x, lambda i, h: d_w.at[:, i, y, :, cols(g, c, 0, *CUT[g][h])],
                   lambda s, h: land1[g].at[0, s, :, :, pl.ds(0, CUT[g][h][1])],
                   back_s.at[4 * g], back_r.at[4 * g]),
            Reduce(y, along_y, lambda i, h: d_w.at[:, x, i, :, cols(g, c, 1, *CUT[g][h])],
                   lambda s, h: land1[g].at[1, s, :, :, pl.ds(0, CUT[g][h][1])],
                   back_s.at[4 * g + 1], back_r.at[4 * g + 1]),
        )

    u_two, t_two, u_one, t_one = back_two_step(0), back_two_step(1), back_one_step(0), back_one_step(1)
    halves = {}

    def kept(g, p):
        return pl.ds(g * 1280 + p * WIDE[g], WIDE[g])

    def send_halves(g, rings):
        for n in range(4):
            for p in range(2):
                ring = rings[p]
                i = (ring.far, ring.right, ring.left, ring.me)[n]
                halves[g, p, n] = remote(
                    piece(d_w, p, i, cols(g, 1 - c, p)), piece(half, p, i, kept(g, p)),
                    half_s.at[g, p, n], half_r.at[g, p, n], sib,
                )
                halves[g, p, n].start()

    def chip_sum(g, rings, p, n):
        halves[g, p, n].wait_recv()
        ring = rings[p]
        i = (ring.far, ring.right, ring.left, ring.me)[n]
        add_into(piece(d_w, p, i, cols(g, c, p)), piece(half, p, i, kept(g, p)))

    send_halves(1, t_two)
    for j in range(2):
        d_out[j] = dot_rows(out_low[local[j], :], inner[...]).astype(bf16)
    give_out = remote(d_out.at[1 - hi], o_out.at[hi], ret_s.at[2], ret_r.at[2], far)
    give_out.start()
    keep_out = pltpu.make_async_copy(d_out.at[hi], o_out.at[hi], keep_s.at[0])
    keep_out.start()

    def toward(n):
        d_att[:, n] = dot(resid[...], wide(shifted(n, 2432))).astype(bf16)

    tiles(3, 256, toward)

    def behind(n, _):
        at = pl.ds(pl.multiple_of(n * 128, 128), 128)
        q2, k2, v2, a2 = q[:, at], k[:, at], v[:, at], d_att[:, at]
        both = a2.astype(f32) * att[:, at].astype(f32)
        dq, dk, dv = [], [], []
        for h in range(2):
            prob = soft[2 * n + h]
            delta = jnp.sum(jnp.where(heads[h], both, 0.0), axis=-1, keepdims=True)
            lift = dot_rows(jnp.where(heads[h], a2, jnp.zeros_like(a2)), v2)
            grad = (prob.astype(f32) * ((lift - delta) * 0.125)).astype(bf16)
            dq.append(dot(grad, k2))
            dk.append(dot_over(grad, q2))
            dv.append(dot_over(prob, a2))
        pick_head = lambda two: jnp.where(heads[0], two[0], two[1])
        dq = pick_head(dq)
        for j in range(2):
            d_q[local[j], at] = turn(dq[j * 128 : (j + 1) * 128], own[j], -1.0).astype(bf16)
        d_kv[:, at] = turn(pick_head(dk), pl.ds(0, 512), -1.0).astype(bf16)
        d_kv[:, shifted(at, 768)] = pick_head(dv).astype(bf16)
        return 0

    lax.fori_loop(0, 1, behind, 0)
    for p in range(2):
        chip_sum(1, t_two, p, 0)
        t_two[p].one()
    lax.fori_loop(1, 2, behind, 0)
    for p in range(2):
        chip_sum(1, t_two, p, 1)
        t_two[p].two()
        chip_sum(1, t_two, p, 2)
        t_two[p].three()
    lax.fori_loop(2, 4, behind, 0)
    for p in range(2):
        t_two[p].pass_right()
        t_two[p].pass_left()
    lax.fori_loop(4, 6, behind, 0)
    for p in range(2):
        chip_sum(1, t_two, p, 3)

    def through(n, _):
        at = pl.ds(pl.multiple_of(n * 256, 256), 256)
        d_one[:, at] = dot_rows(d_kv[...], row_tile(n, pl.ds(896, 1536)))
        for j in range(2):
            d_one[own[j], at] = d_one[own[j], at] + dot_rows(d_q[local[j], :], row_tile(n, pl.ds(128, 768)))
        return 0

    lax.fori_loop(0, 3, through, 0)
    gain_part = dot_over(
        (d_two[...] * normed_two[...]).astype(bf16),
        jnp.broadcast_to((lane == 1).astype(f32).astype(bf16), (256, 128)),
    )
    gain_part += dot_over(
        (d_one[...] * normed_all[...]).astype(bf16),
        jnp.broadcast_to((lane == 0).astype(f32).astype(bf16), (512, 128)),
    )
    put(pl.ds(0, 128), gain_part)
    in_all_t[...] = in_all[...].T
    for j in range(2):
        in_own_t[:, j * 128 : (j + 1) * 128] = in_all[own[j], :].T

    def weights_q(n):
        put(shifted(n, 128), dot(in_own_t[...], d_q[:, n]))

    def weights_kv(n):
        put(shifted(n, 896), dot(in_all_t[...], d_kv[:, n]))

    tiles(3, 256, weights_q)
    tiles(6, 256, weights_kv)
    send_halves(0, u_two)

    def sum_three(to, one, two):
        def row(r, _):
            to[r] = (to[r].astype(f32) + one[r].astype(f32) + two[r].astype(f32)).astype(bf16)
            return 0

        lax.fori_loop(0, 3, row, 0)

    def settle(g, rings, then):
        for p in range(2):
            ring = rings[p]
            ring.landed()
            for h in range(2):
                sum_three(ring.block(ring.me, h), land2[g].at[p, 2 + h], land2[g].at[p, 4 + h])
            then[p].one()
            then[p].two()
            then[p].three()

    settle(1, t_two, t_one)
    for p in range(2):
        chip_sum(0, u_two, p, 0)
        u_two[p].one()
    for p in range(2):
        chip_sum(0, u_two, p, 1)
        u_two[p].two()
        chip_sum(0, u_two, p, 2)
        u_two[p].three()

    def back_one(rows):
        grad, normed = d_one[rows, :], normed_all[rows, :]
        d_one[rows, :] = norm_back(grad * gain_one, normed, inverse_all[rows, 0:1])

    tiles(4, 128, back_one)
    for j in range(2):
        d_one[own[j], :] = d_one[own[j], :] + back_two[local[j], :]

    def leave_rows(b, _):
        rows = pl.ds(pl.multiple_of(b * 128, 128), 128)
        d_tok[b] = dot_rows(d_one[rows, :].astype(bf16), inner[...]).astype(bf16)
        return 0

    lax.fori_loop(0, 4, leave_rows, 0)
    tok_pair = []
    for j in range(2):
        copy = remote(d_tok.at[2 * j + 1 - c], tok_half.at[j], ret_s.at[j], ret_r.at[j], sib)
        copy.start()
        tok_pair.append(copy)

    for p in range(2):
        u_two[p].pass_right()
        u_two[p].pass_left()
    for p in range(2):
        t_one[p].pass_right()
        t_one[p].pass_left()
    for p in range(2):
        chip_sum(0, u_two, p, 3)
    for j in range(2):
        tok_pair[j].wait_recv()
        tok_sum[j] = (d_tok[2 * j + c].astype(f32) + tok_half[j].astype(f32)).astype(bf16)
    give_tok = remote(tok_sum.at[1 - hi], g_out.at[hi], ret_s.at[3], ret_r.at[3], far)
    give_tok.start()
    keep_tok = pltpu.make_async_copy(tok_sum.at[hi], g_out.at[hi], keep_s.at[1])
    keep_tok.start()

    def lay_out(g, rings):
        sf[g][...] = jnp.zeros(sf[g].shape, f32)
        for p in range(2):
            rings[p].landed()
            for r in range(3):
                for h in range(2):
                    at, n = CUT[g][h]
                    total = d_w[r, x, y, :, cols(g, c, p, at, n)].astype(f32)
                    total += land1[g][p, 2 + h, r, :, 0:n].astype(f32)
                    total += land1[g][p, 4 + h, r, :, 0:n].astype(f32)
                    for t in range(n // 128):
                        line = (r * 2 + p) * MANY[g] + at // 128 + t
                        sf[g][pl.ds(line, 16, stride=SIZE[g]), :] = total[:, t * 128 : (t + 1) * 128]
        sb[g][...] = sf[g][...].astype(bf16)

        def push_back(n, _):
            to = lax.rem(z + n, 8)
            remote(
                sb[g].at[owner(g, to * 2, 2)], zbuf[g].at[n], y_s.at[g, n], y_r.at[g, n], device(x, y, to, c)
            ).start()
            return 0

        lax.fori_loop(1, 8, push_back, 0)
        res[g][...] = sf[g][owner(g, z * 2, 2), :]

    ends = []

    def total_up(g):
        def arrive_back(n, _):
            remote(
                sb[g].at[owner(g, z * 2, 2)], zbuf[g].at[n], y_s.at[g, n], y_r.at[g, n],
                device(x, y, lax.rem(z + n, 8), c),
            ).wait()
            res[g][...] = res[g][...] + zbuf[g][n].astype(f32)
            return 0

        lax.fori_loop(1, 8, arrive_back, 0)
        theirs = remote(
            res[g].at[owner(g, 1 - c)], r_out.at[c, part[g]], fin_s.at[g], fin_r.at[g], sib
        )
        theirs.start()
        ours = pltpu.make_async_copy(res[g].at[owner(g, c)], r_out.at[c, part[g]], keep_s.at[2 + g])
        ours.start()
        ends.append((theirs, ours))

    lay_out(1, t_one)
    settle(0, u_two, u_one)
    for p in range(2):
        u_one[p].pass_right()
        u_one[p].pass_left()
    total_up(1)
    lay_out(0, u_one)
    total_up(0)
    for ring in a_one + a_two + b_one + b_two + t_two + t_one + u_two + u_one:
        ring.sent()
    for copy in list(halves.values()) + handed + give + [passed] + tok_pair + [give_out, give_tok]:
        copy.wait_send()
    keep_out.wait()
    keep_tok.wait()
    remote(d_out.at[0], o_out.at[1 - hi], ret_s.at[2], ret_r.at[2], far).wait_recv()
    remote(tok_sum.at[0], g_out.at[1 - hi], ret_s.at[3], ret_r.at[3], far).wait_recv()
    for g in range(2):
        theirs, ours = ends[1 - g]
        ours.wait()
        theirs.wait_send()
        remote(
            res[g].at[owner(g, 0)], r_out.at[1 - c, part[g]], fin_s.at[g], fin_r.at[g], sib
        ).wait_recv()


def block(blk, tok, cot, doc):
    dma = pltpu.SemaphoreType.DMA
    vm = pltpu.VMEM
    return pl.pallas_call(
        block_kernel,
        out_shape=(
            jax.ShapeDtypeStruct((2, 80, 128), f32),
            jax.ShapeDtypeStruct((2, 128, D), bf16),
            jax.ShapeDtypeStruct((2, 128, D), bf16),
        ),
        in_specs=[pl.BlockSpec(memory_space=pltpu.VMEM)] * 4,
        out_specs=[pl.BlockSpec(memory_space=pl.ANY)] * 3,
        scratch_shapes=[
            vm((512, 128), bf16), vm((768, 128), bf16), vm((512, 128), f32), vm((768, 128), f32), vm((128, D), bf16), vm((128, D), bf16),
            vm((4, 128, D), bf16), vm((2, 128, D), bf16),
            vm((3, 4, 4, 16, NC), bf16), vm((3, 4, 4, 16, NC), bf16), vm((3, 4, 4, 16, NC // 2), bf16),
            vm((2, 6, 3, 2, 16, 640), bf16), vm((2, 6, 3, 2, 16, 1024), bf16),
            vm((2, 6, 3, 16, 384), bf16), vm((2, 6, 3, 16, 512), bf16),
            vm((8, 64, 128), bf16), vm((8, 96, 128), bf16), vm((64, 128), f32), vm((96, 128), f32),
            vm((2, 128, D), bf16), vm((4, 128, D), bf16), vm((2, 128, D), bf16), vm((2, 128, D), bf16),
            vm((512, 128), f32), vm((512, 128), f32),
            vm((D, D), bf16), vm((512, D), bf16), vm((512, D), f32), vm((512, 128), f32), vm((512, D), bf16),
            vm((256, D), bf16), vm((512, D), bf16), vm((512, D), bf16), vm((256, 512), f32),
            vm((12, 256, 512), bf16), vm((256, D), bf16), vm((256, D), f32),
            vm((256, D), f32), vm((256, D), bf16), vm((256, D), bf16), vm((256, FF), bf16),
            vm((256, 2 * FF), bf16), vm((256, D), f32), vm((256, D), f32), vm((256, D), bf16),
            vm((256, D), bf16), vm((256, D), bf16), vm((512, 1536), bf16), vm((512, D), f32),
            vm((D, 512), bf16), vm((D, 256), bf16), vm((D, 256), bf16), vm((D, 256), bf16),
            vm((D, 256), bf16), vm((256, D), bf16),
            dma((2,)), dma((2,)), dma((2, 8)), dma((2, 8)), dma((8, 6)), dma((8, 6)), dma((2, 2, 4)), dma((2, 2, 4)),
            dma((2,)), dma((4,)), dma((4,)),
            dma((2, 2, 4)), dma((2, 2, 4)), dma((8, 6)), dma((8, 6)), dma((2, 8)), dma((2, 8)),
            dma((2,)), dma((2,)), dma((4,)), dma((4,)), dma((4,)),
        ],
        compiler_params=pltpu.CompilerParams(
            collective_id=0, has_side_effects=True, vmem_limit_bytes=63 * 2**20
        ),
        name="layer",
    )(blk, tok, cot, doc)


def pack_rows(weights):
    rows = jnp.concatenate(weights, axis=1)
    one = rows[:, :2560].reshape(3, 2, 10, 128).transpose(1, 0, 2, 3).reshape(2, 30, 128)
    two = rows[:, 2560:].reshape(3, 2, 16, 128).transpose(1, 0, 2, 3).reshape(2, 48, 128)
    return jnp.concatenate([jnp.pad(one, ((0, 0), (0, 2), (0, 0))), two], axis=1)


def finish_kernel(rows, out, tok, block_input, cotangent, y_out, g_out, qkv, w_o, w_i, w_d, gains):
    y_out[...] = block_input[...] + out[...].astype(f32)
    g_out[...] = cotangent[...] + tok[...].astype(f32)

    @pl.when(pl.program_id(0) == 0)
    def _():
        for t in range(52):
            core, line, step = (t // 10, t % 10, 10) if t < 20 else ((t - 20) // 16, 32 + (t - 20) % 16, 16)
            to, first = ((gains, 0), (qkv, 1), (w_o, 19), (w_i, 25), (w_d, 43))[
                sum(t >= n for n in (1, 19, 25, 43))
            ]
            at = (t - first) * 128
            for r in range(3):
                to[r : r + 1, at : at + 128] = rows[core, line + r * step : line + r * step + 1, :]


def finish(rows, out, tok, block_input, cotangent):
    one = pl.BlockSpec((1, 128, D), lambda n: (n, 0, 0))
    fixed = lambda *shape: pl.BlockSpec(shape, lambda n: (0,) * len(shape))
    widths = (3 * D, D, 2 * FF, FF, 128)
    return pl.pallas_call(
        finish_kernel,
        grid=(2,),
        out_shape=[jax.ShapeDtypeStruct((2, 128, D), f32)] * 2
        + [jax.ShapeDtypeStruct((3, n), f32) for n in widths],
        in_specs=[fixed(2, 80, 128)] + [one] * 4,
        out_specs=[one] * 2 + [fixed(3, n) for n in widths],
        name="finish",
    )(rows, out, tok, block_input, cotangent)


def body(
    block_input, doc_ids, positions, w_qkv, w_out, w_in, w_down, gain_attn, gain_ffn, cotangent
):
    gains = jnp.pad(jnp.stack([gain_attn, gain_ffn], axis=1), ((0, 0), (0, 126)))
    blk = pack_rows((gains, w_qkv, w_out, w_in, w_down))
    rows, out, tok = block(blk, block_input, cotangent, doc_ids)
    y_out, g_out, d_qkv, d_o, d_in, d_down, d_gain = finish(rows, out, tok, block_input, cotangent)
    return y_out, g_out, d_qkv, d_o, d_in, d_down, d_gain[:, 0], d_gain[:, 1]


def solution(mesh):
    split = P(("dp", "seq"), None)
    both = P("dp", "seq", None)
    return jax.shard_map(
        body,
        mesh=mesh,
        in_specs=(both, P("dp", None), P("dp", "seq"), split, split, split, split,
                  P(("dp", "seq")), P(("dp", "seq")), both),
        out_specs=(both, both, split, split, split, split, P(("dp", "seq")), P(("dp", "seq"))),
        check_vma=False,
    )
```

time: 1070 us -> 131 us (0.12)
  waiting for transfers between devices: 580 us -> 0 us
  blocking collectives: 226 us -> 0 us
  Pallas kernels: 0 us -> 125 us
  local copies, waits for them, and re-layouts: 93.9 us -> 2.24 us
  matrix products: 71.9 us -> 0 us
  starting transfers between devices: 43.8 us -> 0 us
  other arithmetic: 34.1 us -> 2.06 us
  between operations: 15.9 us -> 0.72 us
    all_gather x3 -> x0, waiting for transfers between devices: 499 us -> none  [the longest x1 425 us: in_one_piece(): filled = lax.all_gather(both, axis, axis=dim, tiled=True)]
    unnamed x1 -> x0, blocking collectives: 182 us -> none
    pallas_call x0 -> x2, Pallas kernels: none -> 125 us  [the longest x1 123 us: block(): pl.pallas_call(block_kernel, out_shape=(jax.ShapeDtypeStruct((2, 80, 128)...]
    dot_general x36 -> x0, matrix products: 71.9 us -> none  [the longest x8 22.4 us: over_rows(): lax.dot_general(left, right, (((0,), (0,)), ((), ())), preferred_element_...]
    reduce_scatter x2 -> x0, waiting for transfers between devices: 61.2 us -> none  [sent_together(): lax.psum_scatter(both, axis, scatter_dimension=dim, tiled=True)]
    unnamed x215 -> x10, local copies, waits for them, and re-layouts: 47.2 us -> 1.48 us
    all_gather x4 -> x0, blocking collectives: 44 us -> none  [the longest x2 22.5 us: body(): lax.all_gather(key_here, 'seq', axis=0, tiled=True)]
    all_to_all x9 -> x0, starting transfers between devices: 43.6 us -> none  [the longest x1 10.6 us: sent_and_summed(): lax.all_to_all(cut_along(shard, dim, peers), axis, 0, 0, tiled=True)]
  transfers between devices with their start and end apart: 14 -> 0, of which waited for: 11 -> 0; matrix products, arithmetic and copies ran while one was open for 9% -> 0% of each run, Pallas kernels for 0% -> 0%
where the time goes in v1:
time: 131 us; the launch traced here: 130 us
  Pallas kernels  125 us (95%)
  local copies, waits for them, and re-layouts  2.24 us (2%)
  other arithmetic  2.06 us (2%)
    pallas_call x1, Pallas kernels, block(): pl.pallas_call(block_kernel, out_shape=(jax.ShapeDtypeStruct((2, 80, 128)...  123 us
    pallas_call x1, Pallas kernels, finish(): pl.pallas_call(finish_kernel, grid=(2,), out_shape=[jax.ShapeDtypeStruct(...  2.76 us

profile of v1, /device:TPU:1, one launch (start us, length us, event | category | flops | bytes accessed | tf_op | source)
XLA Modules:
  0.0 130.4 jit_solution(2174543801889877777)
XLA Ops:
  0.6 0.0 copy-start
  0.6 0.7 pad_maximum_fusion.2
  1.3 0.1 copy.24
  1.4 0.0 copy-done
  1.4 0.7 fusion.5
  2.2 0.0 copy-start.1
  2.2 0.0 copy-start.2
  2.3 0.7 copy-done.1
  3.0 0.0 copy-done.2
  3.0 0.6 fusion.1.blk
  3.6 122.6 %layer.1 = (f32[2,80,128]{2,1,0:T(8,128)}, bf16[2,128,768]{2,1,0:T(8,128)(2,1)}, bf16[2,128,768]{2,1,0:T(8,128)(2,1)}) custom-call(bf16[2,80,128]{2,1,0:T(8,128)(2,1)} %fusion.1.blk, f32[2,128,768]{2,1,0:T(8,128)} %block_input.1, f32[2,128,768]{2,1,0:T(8,128)} %cotangent.1, s32[2,512]{1,0:T(2,128)} %doc.1), custom_call_target="tpu_custom_call" | custom-call | tf_op jit(solution)/shard_map/layer/pallas_call | solution.py:786
  126.3 2.8 %finish.1 = (f32[2,128,768]{2,1,0:T(8,128)}, f32[2,128,768]{2,1,0:T(8,128)}, f32[3,2304]{1,0:T(4,128)}, f32[3,768]{1,0:T(4,128)}, f32[3,2304]{1,0:T(4,128)}, /*index=5*/f32[3,1152]{1,0:T(4,128)}, f32[3,128]{1,0:T(4,128)}) custom-call(f32[2,80,128]{2,1,0:T(8,128)} %get-tuple-element.18.rows, bf16[2,128,768]{2,1,0:T(8,128)(2,1)} %get-tuple-element.19.out, ...), custom_call_target="tpu_custom_call" | custom-call | tf_op jit(solution)/shard_map/finish/pallas_call | solution.py:851
  129.0 0.0 copy-start.3
  129.1 0.7 copy-done.3
  129.7 0.7 slice_reduce_fusion
  (6 shorter events, 0.1 us)
Async XLA Ops:
  0.6 0.8 copy-start
  2.2 0.7 copy-start.1
  2.2 0.7 copy-start.2
  129.0 0.7 copy-start.3
